TPU v7x, 32 devices: a whole 2x2x4 slice. The times are simulated.
32 devices in a mesh: gx: 2 (over x), gy: 16 (over z, y, core).
Axes of the slice: x: 2, y: 2, z: 4, core: 2. Of those that a mesh axis runs over, the one named last changes fastest.
Arguments:
- offsets: float32 [3, 4, 32, 2, 128], P(None, 'gx', 'gy'), may hold values from 0 to 1
- velocity: float32 [3, 4, 32, 2, 128], P(None, 'gx', 'gy'), may hold values from -6 to 6
- mass: float32 [4, 32, 2, 128], P('gx', 'gy'), may hold values from 0.00390625 to 0.03125
- energy: float32 [4, 32, 2, 128], P('gx', 'gy'), may hold values from 0.3 to 3
- counts: int32 [4, 32, 2], P('gx', 'gy'), may hold values from 1 to 128
Outputs:
- density: float32 [4, 32, 2, 128], P('gx', 'gy')
- acceleration: float32 [3, 4, 32, 2, 128], P(None, 'gx', 'gy')
- heating: float32 [4, 32, 2, 128], P('gx', 'gy')
Inputs may be any that keep to these rules, and one draw needn't show every extreme that they name: Slots of a cell from counts on hold no particle.
All inputs are finite; a program needn't handle non-finite values.
Results may differ from a plain program's by a relative error of at most 0.0003.
Values sent between devices are 32-bit elements; how exact they have to be, the bound alone decides.
A program may use at most 64 MiB of HBM per device.

v0:
```python
import functools
import math

import jax
import jax.numpy as jnp
from jax import lax
from jax.experimental import pallas as pl
from jax.experimental.pallas import tpu as pltpu
from jax.sharding import PartitionSpec as P

SMOOTHING = 0.5
NORMALISE = 1.0 / (math.pi * 0.125)
ADIABATIC = 5.0 / 3.0
VISC_ALPHA = 1.0
VISC_BETA = 2.0
SOFTENING = 0.01
TINY = 1e-30
VMEM = pltpu.VMEM
MESH = pl.DeviceIdType.MESH
DIRECTIONS = [(dx, dy) for dx in (-1, 0, 1) for dy in (-1, 0, 1) if (dx, dy) != (0, 0)]


def edge(step, count):
    if step == 0:
        return (0, 1, count)
    if step == 1:
        return (count - 1, 0, 1)
    return (0, count + 1, 1)


def start_copies(peers, own_ref, out_ref, count_x, count_y, send_sem, recv_sem):
    copies = []
    for k, (dx, dy) in enumerate(DIRECTIONS):
        from_x, to_x, width_x = edge(dx, count_x)
        from_y, to_y, width_y = edge(dy, count_y)
        copy = pltpu.make_async_remote_copy(
            src_ref=own_ref.at[pl.ds(from_x, width_x), pl.ds(from_y, width_y)],
            dst_ref=out_ref.at[pl.ds(to_x, width_x), pl.ds(to_y, width_y)],
            send_sem=send_sem.at[k],
            recv_sem=recv_sem.at[k],
            device_id=peers[k],
            device_id_type=MESH,
        )
        copy.start()
        copies.append(copy)
    return copies


def segments(x, y, inner_x, inner_y, layers, size_y, own):
    result = []
    for near_x in (x - 1, x, x + 1):
        run = [
            near_y
            for near_y in (y - 1, y, y + 1)
            if (near_x in inner_x and near_y in inner_y) == own
        ]
        for near_y in run:
            first = (near_x * size_y + near_y) * layers
            if result and result[-1][0] + result[-1][1] == first:
                result[-1] = (result[-1][0], result[-1][1] + layers)
            else:
                result.append((first, layers))
    return result


def density_kernel(
    size_gx, size_gy, offsets_hbm, velocity_hbm, mass_hbm, energy_hbm, counts_ref,
    ext_ref, near_ref, part_ref,
    offsets_ref, velocity_ref, mass_ref, energy_ref, own_ref,
    list_ref, pack_ref, total_ref, safe_ref,
    send_sem, recv_sem, rho_send, rho_recv, local_sem, in_sem,
):
    count_x, count_y, layers, _, slots = own_ref.shape
    size_y = count_y + 2
    inner_x, inner_y = range(1, count_x + 1), range(1, count_y + 1)
    own = [(x, y) for x in inner_x for y in inner_y]
    interior = (pl.ds(1, count_x), pl.ds(1, count_y))
    my_x, my_y = lax.axis_index("gx"), lax.axis_index("gy")
    barrier = pltpu.get_barrier_semaphore()
    peers = []
    for dx, dy in DIRECTIONS:
        peers.append(
            (lax.rem(my_x + dx + size_gx, size_gx), lax.rem(my_y + dy + size_gy, size_gy))
        )
    for peer in peers:
        pl.semaphore_signal(barrier, inc=1, device_id=peer, device_id_type=MESH)
    sources = (offsets_hbm, velocity_hbm, mass_hbm, energy_hbm)
    targets = (offsets_ref, velocity_ref, mass_ref, energy_ref)
    loads = [pltpu.make_async_copy(a, b, in_sem.at[k]) for k, (a, b) in enumerate(zip(sources, targets))]
    for load in loads:
        load.start()
    for load in loads:
        load.wait()
    lane = lax.broadcasted_iota(jnp.int32, (1, slots), 1)
    for x in range(count_x):
        for y in range(count_y):
            for z in range(layers):
                at = slice(z, z + 1)
                for f in range(3):
                    own_ref[x, y, z, f : f + 1, :] = offsets_ref[f, x, y, at, :]
                    own_ref[x, y, z, 3 + f : 4 + f, :] = velocity_ref[f, x, y, at, :]
                own_ref[x, y, z, 6:7, :] = jnp.where(
                    lane < counts_ref[x, y, z], mass_ref[x, y, at, :], 0.0
                )
                own_ref[x, y, z, 7:8, :] = energy_ref[x, y, at, :]
    local = pltpu.make_async_copy(own_ref, ext_ref.at[interior], local_sem)
    local.start()
    pl.semaphore_wait(barrier, len(peers))
    copies = start_copies(peers, own_ref, ext_ref, count_x, count_y, send_sem, recv_sem)

    def enter(source, x, y, z, at):
        cell = source[at]
        rows = lax.broadcasted_iota(jnp.int32, cell.shape, 0)
        shift = jnp.where(rows == 0, float(x), jnp.where(rows == 1, float(y), float(z)))
        placed = jnp.where(rows < 3, (cell + shift) * (1.0 / SMOOTHING), cell)
        first = ((x * size_y + y) * layers + z) * slots
        list_ref[first : first + slots, 0:8] = placed.T
        return placed

    def gather(column, runs):
        mine = [
            jnp.concatenate([pack_ref[column, z, f : f + 1, :] for z in range(layers)], axis=1)
            for f in range(3)
        ]

        def body(step, total):
            cell, done = None, 0
            for first, cells in runs:
                here = first + step - done
                cell = here if cell is None else jnp.where(step < done, cell, here)
                done += cells
            near = list_ref[pl.ds(pl.multiple_of(cell * slots, slots), slots), 0:8]
            dist = None
            for f in range(3):
                gap = mine[f] - near[:, f : f + 1]
                dist = gap * gap if dist is None else dist + gap * gap
            q = dist * lax.rsqrt(jnp.maximum(dist, TINY))
            outer = jnp.maximum(2.0 - q, 0.0)
            inner = jnp.maximum(1.0 - q, 0.0)
            kernel = outer * outer * outer - 4.0 * (inner * inner * inner)
            return total + fold(kernel * near[:, 6:7])

        number = sum(cells for _, cells in runs)
        return lax.fori_loop(0, number, body, jnp.zeros((8, layers * slots), jnp.float32))

    for column, (x, y) in enumerate(own):
        for z in range(layers):
            pack_ref[column, z, 0:8, :] = enter(own_ref, x, y, z, (x - 1, y - 1, z))
    for column, (x, y) in enumerate(own):
        runs = segments(x, y, inner_x, inner_y, layers, size_y, True)
        total_ref[column] = gather(column, runs)
    for copy in copies:
        copy.wait()
    for x in range(count_x + 2):
        for y in range(count_y + 2):
            if (x, y) not in own:
                for z in range(layers):
                    enter(ext_ref, x, y, z, (x, y, z))
    for column, (x, y) in enumerate(own):
        runs = segments(x, y, inner_x, inner_y, layers, size_y, False)
        total = total_ref[column] + gather(column, runs)
        value = jnp.sum(total, axis=0, keepdims=True) * (0.25 * NORMALISE)
        for z in range(layers):
            held = own_ref[x - 1, y - 1, z, 6:7, :] > 0.0
            row = value[:, z * slots : (z + 1) * slots]
            safe_ref[x - 1, y - 1, z : z + 1, :] = jnp.where(held, row, 1.0)
    local.wait()
    keep = pltpu.make_async_copy(safe_ref, near_ref.at[interior], local_sem)
    keep.start()
    copies = start_copies(peers, safe_ref, near_ref, count_x, count_y, rho_send, rho_recv)
    for x, y in own:
        for z in range(layers):
            index = (x - 1) * count_y + y - 1
            energy = own_ref[x - 1, y - 1, z, 7:8, :]
            pack_ref[index, z, 7:16, :] = thermal_rows(energy, safe_ref[x - 1, y - 1, z : z + 1, :])
            first = ((x * size_y + y) * layers + z) * slots
            list_ref[first : first + slots, 0:16] = pack_ref[index, z].T
    for column, (x, y) in enumerate(own):
        near_y = [b for b in (y - 1, y, y + 1) if b in inner_y]
        base = (x * size_y + near_y[0]) * layers
        mine = [
            jnp.concatenate([pack_ref[column, z, f : f + 1, :] for z in range(layers)], axis=1)
            for f in range(10)
        ]

        def body(step, sums, base=base, mine=mine):
            row = pl.multiple_of((base + step) * slots, slots)
            near = list_ref[pl.ds(row, slots), 0:16]
            return force_sums(mine, near, near[:, 6:7], sums)

        zeros = tuple(jnp.zeros((8, layers * slots), jnp.float32) for _ in range(4))
        sums = lax.fori_loop(0, len(near_y) * layers, body, zeros)
        for k in range(4):
            part_ref[column, k : k + 1, :] = jnp.sum(sums[k], axis=0, keepdims=True)
        part_ref[column, 4:8, :] = jnp.zeros((4, layers * slots), jnp.float32)
    keep.wait()
    for copy in copies:
        copy.wait()


def thermal_rows(energy, rho):
    return jnp.concatenate(
        [
            (ADIABATIC - 1.0) * energy / rho,
            jnp.sqrt(ADIABATIC * (ADIABATIC - 1.0) * energy) * (0.5 * VISC_ALPHA / VISC_BETA),
            rho * (1.0 / VISC_BETA),
            jnp.zeros((6, energy.shape[1]), jnp.float32),
        ],
        axis=0,
    )


def force_sums(mine, near, mass, sums):
    gaps, dist, approach = [], None, None
    for f in range(3):
        gap = mine[f] - near[:, f : f + 1]
        speed = mine[3 + f] - near[:, 3 + f : 4 + f]
        dist = gap * gap if dist is None else dist + gap * gap
        approach = gap * speed if approach is None else approach + gap * speed
        gaps.append(gap)
    inverse = lax.rsqrt(jnp.maximum(dist, TINY))
    q = dist * inverse
    outer = jnp.maximum(2.0 - q, 0.0)
    slope = jnp.where(q < 1.0, 4.0 - 3.0 * q, outer * outer * inverse)
    closing = jnp.minimum(approach, 0.0)
    soft = dist + SOFTENING
    sound = mine[8] + near[:, 8:9]
    dense = mine[9] + near[:, 9:10]
    half = closing * (closing - sound * soft) / (soft * soft * dense)
    from_own = mine[7] + half
    both = from_own + (near[:, 7:8] + half)
    weight = mass * slope
    push = weight * both
    heat = weight * from_own * approach
    return (
        sums[0] + fold(push * gaps[0]),
        sums[1] + fold(push * gaps[1]),
        sums[2] + fold(push * gaps[2]),
        sums[3] + fold(heat),
    )


def cell_counts(ext_ref, gap):
    size_x, size_y, layers = ext_ref.shape[:3]
    counts, starts, start = {}, {}, jnp.int32(0)
    for x in range(size_x):
        for y in range(size_y):
            for z in range(layers):
                held = jnp.where(ext_ref[x, y, z, 6:7, :] > 0.0, 1.0, 0.0)
                count = jnp.sum(held).astype(jnp.int32)
                counts[x, y, z] = count
                starts[x, y, z] = start
                start = start + (count + 7) // 8 * 8
            starts[x, y, layers] = start
        start = start + gap
    return counts, starts


def base_rows(ext_ref, x, y, z):
    cell = ext_ref[x, y, z]
    rows = lax.broadcasted_iota(jnp.int32, cell.shape, 0)
    shift = jnp.where(rows == 0, float(x), jnp.where(rows == 1, float(y), float(z)))
    placed = (cell + shift) * (1.0 / SMOOTHING)
    return jnp.where(rows < 3, placed, cell)


def fill_lists(features, keys, counts, starts, list_ref, pack_ref, chunk, layers, own):
    for key in keys:
        rows = features(key)
        first = pl.multiple_of(starts[key], 8)
        slots = rows.shape[1]
        list_ref[pl.ds(first, slots), 0 : rows.shape[0]] = rows.T
        if key[1:] == keys[-1][1:]:
            after = pl.multiple_of(first + slots, 8)
            list_ref[pl.ds(after, chunk), :] = jnp.zeros((chunk, list_ref.shape[1]), jnp.float32)
    for column, (x, y) in enumerate(own):
        lower, upper = features((x, y, 0)), features((x, y, 1))
        rolled = pltpu.roll(upper, jnp.bitwise_and(counts[x, y, 0], 127), 1)
        lane = lax.broadcasted_iota(jnp.int32, lower.shape, 1)
        pack_ref[column, 0] = jnp.where(lane < counts[x, y, 0], lower, rolled)
        pack_ref[column, 1] = rolled


def sweep(pair_body, n_sums, block_list, starts, x, y, inner_y, layers, chunk):
    spans = []
    for near_x in (x - 1, x, x + 1):
        skip = inner_y if near_x == x else ()
        for near_y in (y - 1, y, y + 1):
            if near_y in skip:
                continue
            first, end = starts[near_x, near_y, 0], starts[near_x, near_y, layers]
            if spans and spans[-1][0] == (near_x, near_y - 1):
                spans[-1] = ((near_x, near_y), spans[-1][1], end)
            else:
                spans.append(((near_x, near_y), first, end))
    total, below = jnp.int32(0), []
    for _, first, end in spans:
        below.append(total)
        total = total + (end - first + (chunk - 1)) // chunk

    def body(step, sums):
        row, last = spans[0][1] + step * chunk, spans[0][2]
        for before, (_, first, end) in zip(below[1:], spans[1:]):
            row = jnp.where(step < before, row, first + (step - before) * chunk)
            last = jnp.where(step < before, last, end)
        return pair_body(pl.multiple_of(row, 8), last, sums)

    width = 128 * block_list
    zeros = tuple(jnp.zeros((8, width), jnp.float32) for _ in range(n_sums))
    sums = lax.fori_loop(0, total, body, zeros)
    return [jnp.sum(s, axis=0, keepdims=True) for s in sums]


def fold(values):
    return jnp.sum(values.reshape(values.shape[0] // 8, 8, values.shape[1]), axis=0)


def unpack(row_a, row_b, count):
    back = jnp.bitwise_and(128 - jnp.bitwise_and(count, 127), 127)
    a = pltpu.roll(jnp.broadcast_to(row_a, (8, 128)), back, 1)[0:1]
    b = pltpu.roll(jnp.broadcast_to(row_b, (8, 128)), back, 1)[0:1]
    lane = lax.broadcasted_iota(jnp.int32, (1, 128), 1)
    upper = jnp.where(lane < 128 - count, a, b)
    return row_a, upper


def run_column(make_body, n_sums, total, out_ref, starts, x, y, inner_y, layers, chunks):
    @pl.when(total > 128)
    def _():
        sums = sweep(make_body(2, chunks[1]), n_sums, 2, starts, x, y, inner_y, layers, chunks[1])
        for k, row in enumerate(sums):
            out_ref[k : k + 1, :] = row

    @pl.when(total <= 128)
    def _():
        sums = sweep(make_body(1, chunks[0]), n_sums, 1, starts, x, y, inner_y, layers, chunks[0])
        for k, row in enumerate(sums):
            out_ref[k : k + 1, 0:128] = row
            out_ref[k : k + 1, 128:256] = jnp.zeros_like(row)


def own_columns(ext_ref):
    return [
        (x, y) for x in range(1, ext_ref.shape[0] - 1) for y in range(1, ext_ref.shape[1] - 1)
    ]


def all_cells(ext_ref):
    size_x, size_y, layers = ext_ref.shape[:3]
    return [(x, y, z) for x in range(size_x) for y in range(size_y) for z in range(layers)]


def wide(pack_ref, column, blocks, row):
    parts = [pack_ref[column, b, row : row + 1, :] for b in range(blocks)]
    return parts[0] if blocks == 1 else jnp.concatenate(parts, axis=1)


def force_kernel(
    chunks, ext_ref, rho_ref, part_ref, density_ref, accel_ref, heat_ref, feat_ref, list_ref, pack_ref, sum_ref
):
    layers = ext_ref.shape[2]
    counts, starts = cell_counts(ext_ref, max(chunks))
    own = own_columns(ext_ref)
    inner_y = range(1, ext_ref.shape[1] - 1)

    for key in all_cells(ext_ref):
        x, y, z = key
        energy = ext_ref[x, y, z, 7:8, :]
        rho = rho_ref[x, y, z : z + 1, :]
        feat_ref[x, y, z, 0:8, :] = base_rows(ext_ref, x, y, z)
        feat_ref[x, y, z, 7:16, :] = thermal_rows(energy, rho)
    fill_lists(
        lambda key: feat_ref[key],
        all_cells(ext_ref), counts, starts, list_ref, pack_ref, max(chunks), layers, own,
    )
    for column, (x, y) in enumerate(own):

        def make_body(blocks, chunk, column=column):
            mine = [wide(pack_ref, column, blocks, f) for f in range(10)]

            def body(row, end, sums):
                near = list_ref[pl.ds(row, chunk), 0:16]
                place = lax.broadcasted_iota(jnp.int32, near.shape, 0)
                mass = jnp.where(place < end - row, near, 0.0)[:, 6:7]
                return force_sums(mine, near, mass, sums)

            return body

        count = counts[x, y, 0]
        run_column(
            make_body, 4, count + counts[x, y, 1], sum_ref, starts, x, y, inner_y, layers, chunks
        )
        for z in range(layers):
            held = ext_ref[x, y, z, 6:7, :] > 0.0
            density_ref[x - 1, y - 1, z : z + 1, :] = jnp.where(held, rho_ref[x, y, z : z + 1, :], 0.0)
        factor = 0.75 * NORMALISE / SMOOTHING
        for k in range(4):
            rows = unpack(sum_ref[k : k + 1, 0:128], sum_ref[k : k + 1, 128:256], count)
            for z in range(layers):
                held = ext_ref[x, y, z, 6:7, :] > 0.0
                value = rows[z] + part_ref[column, k : k + 1, z * 128 : (z + 1) * 128]
                if k < 3:
                    accel_ref[k, x - 1, y - 1, z : z + 1, :] = jnp.where(held, value * factor, 0.0)
                else:
                    heat_ref[x - 1, y - 1, z : z + 1, :] = jnp.where(held, value * -factor, 0.0)


def shards(offsets, velocity, mass, energy, counts):
    slots = mass.shape[-1]
    count_x, count_y, layers = mass.shape[:3]
    wide_x, wide_y = count_x + 2, count_y + 2
    cells = wide_x * wide_y * layers
    own = count_x * count_y
    vmem = pl.BlockSpec(memory_space=VMEM)
    sems = pltpu.SemaphoreType.DMA((len(DIRECTIONS),))
    own_shape = (count_x, count_y, layers, 8, slots)
    extended, near, part = pl.pallas_call(
        functools.partial(density_kernel, lax.axis_size("gx"), lax.axis_size("gy")),
        out_shape=[
            jax.ShapeDtypeStruct((wide_x, wide_y) + own_shape[2:], jnp.float32),
            jax.ShapeDtypeStruct((wide_x, wide_y, layers, slots), jnp.float32),
            jax.ShapeDtypeStruct((own, 8, layers * slots), jnp.float32),
        ],
        in_specs=[pl.BlockSpec(memory_space=pl.ANY)] * 4 + [pl.BlockSpec(memory_space=pltpu.SMEM)],
        out_specs=[vmem, vmem, vmem],
        scratch_shapes=[
            VMEM(offsets.shape, jnp.float32),
            VMEM(velocity.shape, jnp.float32),
            VMEM(mass.shape, jnp.float32),
            VMEM(energy.shape, jnp.float32),
            VMEM(own_shape, jnp.float32),
            VMEM((cells * slots, 128), jnp.float32),
            VMEM((own, layers, 16, slots), jnp.float32),
            VMEM((own, 8, layers * slots), jnp.float32),
            VMEM((count_x, count_y, layers, slots), jnp.float32),
            sems,
            sems,
            sems,
            sems,
            pltpu.SemaphoreType.DMA,
            pltpu.SemaphoreType.DMA((4,)),
        ],
        compiler_params=pltpu.CompilerParams(collective_id=0, has_side_effects=True),
        name="density",
    )(offsets, velocity, mass, energy, counts)
    force_chunks = (128, 64)
    density, accel, heat = pl.pallas_call(
        functools.partial(force_kernel, force_chunks),
        out_shape=[
            jax.ShapeDtypeStruct(mass.shape, jnp.float32),
            jax.ShapeDtypeStruct((3,) + mass.shape, jnp.float32),
            jax.ShapeDtypeStruct(mass.shape, jnp.float32),
        ],
        in_specs=[vmem, vmem, vmem],
        out_specs=[vmem, vmem, vmem],
        scratch_shapes=[
            VMEM((wide_x, wide_y, layers, 16, slots), jnp.float32),
            VMEM((cells * slots + wide_x * max(force_chunks), 128), jnp.float32),
            VMEM((own, 2, 16, slots), jnp.float32),
            VMEM((8, 2 * slots), jnp.float32),
        ],
        name="force",
    )(extended, near, part)
    return (density, accel, heat)


def solution(mesh):
    in_specs = (
        P(None, "gx", "gy", None, None),
        P(None, "gx", "gy", None, None),
        P("gx", "gy", None, None),
        P("gx", "gy", None, None),
        P("gx", "gy", None),
    )
    out_specs = (
        P("gx", "gy", None, None),
        P(None, "gx", "gy", None, None),
        P("gx", "gy", None, None),
    )
    return jax.shard_map(shards, mesh=mesh, in_specs=in_specs, out_specs=out_specs, check_vma=False)
```

profile of v0, /device:TPU:0, one launch (start us, length us, event | category | flops | bytes accessed | tf_op | source)
XLA Modules:
  0.0 44.1 jit_solution(8847276591134166212)
XLA Ops:
  0.6 28.3 %density.1 = (f32[4,4,2,8,128]{4,3,2,1,0:T(8,128)}, f32[4,4,2,128]{3,2,1,0:T(2,128)}, f32[4,8,256]{2,1,0:T(8,128)}) custom-call(f32[3,2,2,2,128]{4,3,2,1,0:T(2,128)} %offsets_hbm.1, f32[3,2,2,2,128]{4,3,2,1,0:T(2,128)} %velocity_hbm.1, f32[2,2,2,128]{3,2,1,0:T(2,128)} %mass_hbm.1, f32[2,2,2,128]{3,2,1,0:T(2,128)} %energy_hbm.1, s32[2,2,2]{2,1,0:T(2,128)} %counts_ref.1), custom_call_target="tpu_custom_call" | custom-call | tf_op jit(solution)/shard_map/density/pallas_call | solution.py:417
  28.9 15.1 %force.1 = (f32[2,2,2,128]{3,2,1,0:T(2,128)}, f32[3,2,2,2,128]{4,3,2,1,0:T(2,128)}, f32[2,2,2,128]{3,2,1,0:T(2,128)}) custom-call(f32[4,4,2,8,128]{4,3,2,1,0:T(8,128)} %get-tuple-element.6.ext_ref, f32[4,4,2,128]{3,2,1,0:T(2,128)} %get-tuple-element.7.rho_ref, f32[4,8,256]{2,1,0:T(8,128)} %get-tuple-element.8.part_ref), custom_call_target="tpu_custom_call" | custom-call | tf_op jit(solution)/shard_map/force/pallas_call | solution.py:447
where the time goes:
time: 44.1 us
  Pallas kernels  43.4 us (98%)
  between operations  0.64 us (1%)
    pallas_call x1, Pallas kernels, shards(): pl.pallas_call(functools.partial(density_kernel, lax.axis_size('gx'), lax...  28.3 us
    pallas_call x1, Pallas kernels, shards(): pl.pallas_call(functools.partial(force_kernel, force_chunks), out_shape=[...  15.1 us

commit v1 on v0

--- a/solution.py
+++ b/solution.py
@@ -126,10 +126,11 @@
         def body(step, total):
             cell, done = None, 0
             for first, cells in runs:
-                here = first + step - done
+                here = first // layers + step - done
                 cell = here if cell is None else jnp.where(step < done, cell, here)
-                done += cells
-            near = list_ref[pl.ds(pl.multiple_of(cell * slots, slots), slots), 0:8]
+                done += cells // layers
+            rows = layers * slots
+            near = list_ref[pl.ds(pl.multiple_of(cell * rows, rows), rows), 0:8]
             dist = None
             for f in range(3):
                 gap = mine[f] - near[:, f : f + 1]
@@ -140,7 +141,7 @@
             kernel = outer * outer * outer - 4.0 * (inner * inner * inner)
             return total + fold(kernel * near[:, 6:7])
 
-        number = sum(cells for _, cells in runs)
+        number = sum(cells // layers for _, cells in runs)
         return lax.fori_loop(0, number, body, jnp.zeros((8, layers * slots), jnp.float32))
 
     for column, (x, y) in enumerate(own):

time: 44.1 us -> 39 us (0.88)
  Pallas kernels: 43.4 us -> 38 us
    pallas_call x1, Pallas kernels: 28.3 us -> 25.5 us  [shards(): pl.pallas_call(functools.partial(density_kernel, lax.axis_size('gx'), lax...]
    pallas_call x1, Pallas kernels: 15.1 us -> 12.5 us  [shards(): pl.pallas_call(functools.partial(force_kernel, force_chunks), out_shape=[...]
where the time goes in v1:
time: 39 us; the launch traced here: 38.6 us
  Pallas kernels  38 us (97%)
  between operations  0.64 us (2%)
    pallas_call x1, Pallas kernels, shards(): pl.pallas_call(functools.partial(density_kernel, lax.axis_size('gx'), lax...  25.5 us
    pallas_call x1, Pallas kernels, shards(): pl.pallas_call(functools.partial(force_kernel, force_chunks), out_shape=[...  12.5 us

profile of v1, /device:TPU:0, one launch (start us, length us, event | category | flops | bytes accessed | tf_op | source)
XLA Modules:
  0.0 38.6 jit_solution(2760100876971970308)
XLA Ops:
  0.6 25.5 %density.1 = (f32[4,4,2,8,128]{4,3,2,1,0:T(8,128)}, f32[4,4,2,128]{3,2,1,0:T(2,128)}, f32[4,8,256]{2,1,0:T(8,128)}) custom-call(f32[3,2,2,2,128]{4,3,2,1,0:T(2,128)} %offsets_hbm.1, f32[3,2,2,2,128]{4,3,2,1,0:T(2,128)} %velocity_hbm.1, f32[2,2,2,128]{3,2,1,0:T(2,128)} %mass_hbm.1, f32[2,2,2,128]{3,2,1,0:T(2,128)} %energy_hbm.1, s32[2,2,2]{2,1,0:T(2,128)} %counts_ref.1), custom_call_target="tpu_custom_call" | custom-call | tf_op jit(solution)/shard_map/density/pallas_call | solution.py:418
  26.1 12.5 %force.1 = (f32[2,2,2,128]{3,2,1,0:T(2,128)}, f32[3,2,2,2,128]{4,3,2,1,0:T(2,128)}, f32[2,2,2,128]{3,2,1,0:T(2,128)}) custom-call(f32[4,4,2,8,128]{4,3,2,1,0:T(8,128)} %get-tuple-element.6.ext_ref, f32[4,4,2,128]{3,2,1,0:T(2,128)} %get-tuple-element.7.rho_ref, f32[4,8,256]{2,1,0:T(8,128)} %get-tuple-element.8.part_ref), custom_call_target="tpu_custom_call" | custom-call | tf_op jit(solution)/shard_map/force/pallas_call | solution.py:448
